TPU v7x, 128 devices: a whole 4x4x4 slice. The times are simulated.
128 devices in a mesh: seq: 16 (over y, z), batch: 8 (over x, core).
Axes of the slice: x: 4, y: 4, z: 4, core: 2. Of those that a mesh axis runs over, the one named last changes fastest.
Arguments:
- q_nope: bfloat16 [8, 64, 128, 128], P('batch', None, 'seq'), may hold values from -6 to 6
- q_rope: bfloat16 [8, 64, 128, 64], P('batch', None, 'seq'), may hold values from -8 to 8
- absorb_k: bfloat16 [128, 128, 512], P('seq'), may hold values from -0.5 to 0.5
- absorb_v: bfloat16 [128, 512, 128], P('seq'), may hold values from -0.25 to 0.25
- cache_latent: bfloat16 [8, 16384, 512], P('batch', 'seq'), may hold values from -6 to 6
- cache_rope: bfloat16 [8, 16384, 64], P('batch', 'seq'), may hold values from -8 to 8
- draft_latent: bfloat16 [8, 64, 512], P('batch'), may hold values from -6 to 6
- draft_rope: bfloat16 [8, 64, 64], P('batch'), may hold values from -6 to 6
- residual: bfloat16 [512, 7168], P('batch', 'seq'), may hold values from -1.2 to 1.2
- out_proj: bfloat16 [16384, 7168], P('seq'), may hold values from -0.046875 to 0.046875
- norm_gain: float32 [7168], replicated, may hold values from 0.5 to 1.5
- lm_head: bfloat16 [65536, 7168], P(('seq', 'batch')), may hold values from -2.4095235 to 2.4095235
- parent: int32 [8, 64], replicated, may hold values from 0 to 62, as said below
- draft_ids: int32 [8, 64], replicated, may hold values from 0 to 65535
- cache_len: int32 [8], P('batch'), may hold values from 4096 to 16384
- accept_len: int32 [8], P('batch'), may hold values from 1 to 64
Outputs:
- hidden_out: bfloat16 [512, 7168], P('batch', 'seq')
- target_logp: float32 [8, 64], P('batch')
- accepted_score: float32 [8], P('batch')
Inputs may be any that keep to these rules, and one draw needn't show every extreme that they name: parent[b, 0] = 0, and 0 <= parent[b, i] < i for i >= 1.
All inputs are finite; a program needn't handle non-finite values.
Results may differ from a plain program's by a relative error of at most 0.0095.
Values may be sent and summed in bfloat16 or wider, within the bound.
A program may use at most 256 MiB of HBM per device.

v0:
```python
import math
import jax
import jax.numpy as jnp
from jax import lax
from jax.sharding import Mesh
from jax.sharding import PartitionSpec as P

SEQ = ("seq_0", "seq_1")
BATCH = ("batch_0", "batch_1")
SEQ_BATCH = ("seq_0", "seq_1", "batch_0", "batch_1")
masked_value = -1e30
norm_epsilon = 1e-06
highest = lax.Precision.HIGHEST


def sent_together(arrays, axis, dim, along):
    ends, at = ([], 0)
    for a in arrays[:-1]:
        at += a.shape[along]
        ends.append(at)
    both = jnp.concatenate(arrays, axis=along)
    return tuple(jnp.split(lax.all_gather(both, axis, axis=dim, tiled=True), ends, axis=along))


def copy_for_each(array, axis):
    copies = jnp.broadcast_to(array, (lax.axis_size(axis), *array.shape))
    return lax.all_to_all(copies, axis, split_axis=0, concat_axis=0, tiled=True)


def over_copies(array, axis):
    everything = copy_for_each(array, axis)
    return jnp.max(everything, axis=0)


def gathered_once(array, axis):
    leaves = jax.tree.leaves(array)
    sequence = sorted(range(len(leaves)), key=lambda k: -leaves[k].size)
    width = (1, *leaves[sequence[0]].shape)[-1]
    lines = [
        jnp.pad(leaves[k].reshape(-1), (0, -leaves[k].size % width)).reshape(-1, width)
        for k in sequence
    ]
    both, at, found = (lax.all_gather(jnp.concatenate(lines), axis), 0, {})
    for k, line in zip(sequence, lines):
        piece = both[:, at : at + len(line)].reshape(len(both), -1)
        found[k] = piece[:, : leaves[k].size].reshape(-1, *leaves[k].shape)
        at += len(line)
    numbers = iter(range(len(leaves)))
    return jax.tree.map(lambda _: found[next(numbers)], array)


def combined_by_axis(array, axes, combine):
    for axis in axes:
        pieces = gathered_once(array, axis)
        array = jax.tree.map(lambda part: part[0], pieces)
        for k in range(1, lax.axis_size(axis)):
            array = combine(array, jax.tree.map(lambda part: part[k], pieces))
    return array


def ancestry_of(parents):
    draft_count = parents.shape[1]
    indices = jnp.arange(draft_count, dtype=jnp.int32)
    parent_map = (
        (parents[:, :, None] == indices[None, None, :]) & (indices[None, :, None] > 0)
    ).astype(jnp.float32)
    ancestry = jnp.broadcast_to(jnp.eye(draft_count, dtype=jnp.float32), parent_map.shape)
    for doubling in range(draft_count.bit_length() - 1):
        ancestry = ancestry + jnp.einsum("rij,rjk->rik", ancestry, parent_map, precision=highest)
        parent_map = jnp.einsum("rij,rjk->rik", parent_map, parent_map, precision=highest)
    return ancestry > 0.5


def combine_soft(earlier, later):
    top_new = jnp.maximum(earlier[0], later[0])
    mass_new = earlier[1] * jnp.exp(earlier[0] - top_new) + later[1] * jnp.exp(later[0] - top_new)
    return (top_new, mass_new, earlier[2] + later[2])


def body(
    q_nope,
    q_rope,
    absorb_k,
    absorb_v,
    cache_latent,
    cache_rope,
    draft_latent,
    draft_rope,
    residual,
    out_proj,
    norm_gain,
    lm_head,
    parent,
    draft_ids,
    cache_len,
    accept_len,
):
    requests, draft_count, local_heads, nope_width = q_nope.shape
    cache_rows = cache_latent.shape[1]
    score_scale = 1.0 / math.sqrt(nope_width + q_rope.shape[3])
    seq_index = lax.axis_index(SEQ)
    batch_index = lax.axis_index(BATCH)
    query_latent = jnp.einsum(
        "rihn,hnc->rihc", q_nope, absorb_k, preferred_element_type=jnp.float32
    ).astype(jnp.bfloat16)
    query_all, rope_all = sent_together((query_latent, q_rope), SEQ, 2, 3)
    cache_scores = jnp.einsum(
        "rihc,rtc->rhit", query_all, cache_latent, preferred_element_type=jnp.float32
    )
    cache_scores = cache_scores + jnp.einsum(
        "rihe,rte->rhit", rope_all, cache_rope, preferred_element_type=jnp.float32
    )
    positions = seq_index * cache_rows + jnp.arange(cache_rows, dtype=jnp.int32)
    in_cache = positions[None, :] < cache_len[:, None]
    cache_scores = jnp.where(in_cache[:, None, None, :], cache_scores * score_scale, masked_value)
    tree_scores = jnp.einsum(
        "rihc,rjc->rhij", query_all, draft_latent, preferred_element_type=jnp.float32
    )
    tree_scores = tree_scores + jnp.einsum(
        "rihe,rje->rhij", rope_all, draft_rope, preferred_element_type=jnp.float32
    )
    own_parents = lax.dynamic_slice_in_dim(parent, batch_index * requests, requests, 0)
    ancestry = ancestry_of(own_parents)
    tree_scores = jnp.where(ancestry[:, None, :, :], tree_scores * score_scale, masked_value)
    local_top = jnp.maximum(jnp.max(cache_scores, axis=3), jnp.max(tree_scores, axis=3))
    row_top = over_copies(local_top, SEQ)
    cache_weights = jnp.exp(cache_scores - row_top[..., None])
    weight_sum = jnp.sum(cache_weights, axis=3)
    partial_value = jnp.einsum(
        "rhit,rtc->rhic",
        cache_weights.astype(jnp.bfloat16),
        cache_latent,
        preferred_element_type=jnp.float32,
    )
    head_first = seq_index * local_heads
    tree_mine = lax.dynamic_slice_in_dim(tree_scores, head_first, local_heads, 1)
    top_mine = lax.dynamic_slice_in_dim(row_top, head_first, local_heads, 1)
    tree_weights = jnp.exp(tree_mine - top_mine[..., None])
    tree_out = jnp.einsum(
        "rhij,rjc->rhic",
        tree_weights.astype(jnp.bfloat16),
        draft_latent,
        preferred_element_type=jnp.float32,
    )
    latent_sum, weight_total = (
        lax.psum_scatter(partial_value, SEQ, scatter_dimension=1, tiled=True),
        lax.psum_scatter(weight_sum, SEQ, scatter_dimension=1, tiled=True),
    )
    summed = jnp.einsum(
        "rhic,hcn->rhin", latent_sum + tree_out, absorb_v, preferred_element_type=jnp.float32
    )
    weight_total = weight_total + jnp.sum(tree_weights, axis=3)
    head_out = (summed / weight_total[..., None]).astype(jnp.bfloat16)
    head_rows = jnp.transpose(head_out, (0, 2, 1, 3)).reshape(
        requests * draft_count, local_heads * head_out.shape[3]
    )
    branch_term = jnp.dot(head_rows, out_proj, preferred_element_type=jnp.float32)
    width_local = residual.shape[1]
    feature_first = seq_index * width_local
    residual_wide = lax.dynamic_update_slice_in_dim(
        jnp.zeros_like(branch_term), residual.astype(jnp.float32), feature_first, 1
    )
    stream = lax.psum(branch_term + residual_wide, SEQ)
    square = jnp.sum(stream * stream, axis=1)
    normed = (
        stream * lax.rsqrt(square / stream.shape[1] + norm_epsilon)[:, None] * norm_gain
    ).astype(jnp.bfloat16)
    hidden_out = lax.dynamic_slice_in_dim(stream, feature_first, width_local, 1).astype(
        jnp.bfloat16
    )
    vocab_rows = lm_head.shape[0]
    vocab_first = lax.axis_index(SEQ_BATCH) * vocab_rows
    logits = jnp.einsum(
        "rd,vd->rv",
        lax.all_gather(normed, BATCH, axis=0, tiled=True),
        lm_head,
        preferred_element_type=jnp.float32,
    )
    request_total = parent.shape[0]
    parent_rows = (
        jnp.arange(request_total, dtype=jnp.int32)[:, None] * draft_count + parent
    ).reshape(-1)
    source = logits[parent_rows]
    column = jnp.arange(vocab_rows, dtype=jnp.int32) + vocab_first
    picked = jnp.sum(
        jnp.where(column[None, :] == draft_ids.reshape(-1)[:, None], source, 0.0), axis=1
    )
    local_best = jnp.max(logits, axis=1)
    local_mass = jnp.sum(jnp.exp(logits - local_best[:, None]), axis=1)
    best, exp_mass, chosen = combined_by_axis(
        (local_best, local_mass, picked), SEQ_BATCH, combine_soft
    )
    log_total = best + jnp.log(exp_mass)
    target_all = (chosen - log_total[parent_rows]).reshape(request_total, draft_count)
    target_logp = lax.dynamic_slice_in_dim(target_all, batch_index * requests, requests, 0)
    accepted_score = jnp.sum(
        jnp.where(
            jnp.arange(draft_count, dtype=jnp.int32)[None, :] < accept_len[:, None],
            target_logp,
            0.0,
        ),
        axis=1,
    )
    return (hidden_out, target_logp, accepted_score)


def solution(mesh):
    split = Mesh(mesh.devices.reshape(4, 4, 4, 2), ("seq_0", "seq_1", "batch_0", "batch_1"))
    in_specs = (
        P(BATCH, None, SEQ, None),
        P(BATCH, None, SEQ, None),
        P(SEQ, None, None),
        P(SEQ, None, None),
        P(BATCH, SEQ, None),
        P(BATCH, SEQ, None),
        P(BATCH, None, None),
        P(BATCH, None, None),
        P(BATCH, SEQ),
        P(SEQ, None),
        P(),
        P(SEQ_BATCH, None),
        P(),
        P(),
        P(BATCH),
        P(BATCH),
    )
    out_specs = (P(BATCH, SEQ), P(BATCH, None), P(BATCH))
    return jax.shard_map(body, mesh=split, in_specs=in_specs, out_specs=out_specs, check_vma=False)
```

profile of v0, /device:TPU:1, one launch (start us, length us, event | category | flops | bytes accessed | tf_op | source)
XLA Modules:
  0.0 529.6 jit_solution(17929896783594325636)
XLA Ops:
  7.2 1.0 copy.41
  8.2 1.6 fusion.16
  9.9 0.9 maximum_bitcast_fusion
  11.5 0.7 fusion.88
  12.2 0.2 fusion.39
  12.5 0.2 convolution_add_fusion.5
  12.7 0.2 fusion.99
  12.8 0.2 convolution_add_fusion.4
  13.0 0.2 fusion.100
  13.2 0.2 convolution_add_fusion.3
  13.3 0.2 fusion.101
  13.5 0.2 convolution_add_fusion.2
  13.7 0.2 fusion.102
  13.9 0.2 convolution_add_fusion.1
  14.0 0.2 fusion.17
  14.2 0.1 copy.45
  14.3 80.4 %all-gather.11.cloned.1.call-done = bf16[1,64,128,576]{3,1,0,2:T(8,128)(2,1)} async-done(((bf16[1,64,8,576]{3,1,0,2:T(8,128)(2,1)}), bf16[1,64,128,576]{3,1,0,2:T(8,128)(2,1)}) %all-gather.11.cloned.1.call-update) | async-done | bytes 9437200 | tf_op jit(solution)/shard_map/all_gather | solution.py:22
  94.7 1.8 split.9
  96.5 2.9 copy.69
  99.4 7.5 %fusion.10 = f32[64,128,64]{0,2,1:T(8,128)S(1)} fusion(bf16[1,64,512]{2,1,0:T(8,128)(2,1)S(1)} %copy-done.5, bf16[1,64,128,576]{3,1,0,2:T(8,128)(2,1)} %all-gather.11.cloned.1.call-done), kind=kOutput, calls=%fused_computation.11 | convolution fusion | flops 536870912 | bytes 10551296 | tf_op jit(solution)/shard_map/rihc,rjc->rhij/dot_general | solution.py:116
  106.9 5.8 %fusion.97 = (f32[128,64]{1,0:T(8,128)S(1)}, f32[1,128,64,64]{2,3,1,0:T(8,128)}) fusion(f32[64,128,64]{0,2,1:T(8,128)S(1)} %fusion.10, bf16[1,64,64]{2,1,0:T(8,128)(2,1)S(1)} %copy-done.8, bf16[1,64,128,576]{3,1,0,2:T(8,128)(2,1)} %all-gather.11.cloned.1.call-done, pred[64,64]{0,1:T(8,128)(4,1)S(1)} %copy.45), kind=kOutput, calls=%fused_computation.169 | convolution fusion | flops 69197824 | bytes 6336512 | tf_op jit(solution)/shard_map/rihe,rje->rhij/dot_general | solution.py:119
  112.8 7.7 %split.8 = bf16[1,64,128,512]{3,1,0,2:T(8,128)(2,1)} slice(bf16[1,64,128,576]{3,1,0,2:T(8,128)(2,1)} %all-gather.11.cloned.1.call-done), slice={[0:1], [0:64], [0:128], [0:512]} | slice | bytes 16777216 | tf_op jit(solution)/shard_map/split | solution.py:22
  120.5 30.0 %fusion.12 = f32[64,128,1024]{2,1,0:T(8,128)} fusion(bf16[1,64,128,512]{3,1,0,2:T(8,128)(2,1)} %split.8, bf16[1,1024,512]{2,1,0:T(8,128)(2,1)S(1)} %copy-done), kind=kOutput, calls=%fused_computation.14 | convolution fusion | flops 8589934592 | bytes 42991616 | tf_op jit(solution)/shard_map/rihc,rtc->rhit/dot_general | solution.py:107
  150.5 21.9 %fusion.96 = (f32[128,64]{0,1:T(8,128)S(1)}, f32[1,128,64,1024]{3,1,2,0:T(8,128)}) fusion(f32[64,128,1024]{2,1,0:T(8,128)} %fusion.12, bf16[1,1024,64]{1,2,0:T(8,128)(2,1)S(1)} %copy-done.4, bf16[1,64,128,64]{2,3,1,0:T(8,128)(2,1)S(1)} %copy-done.3, pred[1024]{0:T(1024)(128)(4,1)S(1)} %add_compare_fusion), kind=kOutput, calls=%fused_computation.168 | convolution fusion | flops 1107288064 | bytes 68322304 | tf_op jit(solution)/shard_map/rihe,rte->rhit/dot_general | solution.py:110
  172.5 15.1 %all_to_all.5 = f32[16,1,128,64]{2,3,1,0:T(8,128)S(1)} all-to-all(f32[16,1,128,64]{2,3,1,0:T(8,128)S(1)} %broadcast_in_dim.37), channel_id=1, replica_groups=mesh['seq_0'=4,'seq_1'=4,'batch_0'=4,'batch_1'=2] {'seq_0','seq_1'}, dimensions={0} | all-to-all | bytes 1048576 | tf_op jit(solution)/shard_map/all_to_all | solution.py:27
  187.7 18.7 %fusion.7 = f32[1,128,64,512]{3,1,2,0:T(8,128)} fusion(f32[1,128,64,1024]{3,1,2,0:T(8,128)} %get-tuple-element.19, f32[128,64]{0,1:T(8,128)S(1)} %reduce_max.38, bf16[1,1024,512]{2,1,0:T(8,128)(2,1)S(1)} %copy-done), kind=kOutput, calls=%fused_computation.10 | convolution fusion | flops 8606711808 | bytes 51412992 | tf_op jit(solution)/shard_map/rhit,rtc->rhic/dot_general | solution.py:129
  206.5 0.6 copy-done.12
  207.0 0.6 dynamic-slice.5
  208.3 0.1 constant_dynamic-slice_fusion.1
  208.4 1.0 fusion.24
  209.4 0.1 copy.67
  209.5 14.9 %fusion.1 = f32[128,64]{0,1:T(8,128)S(1)} fusion(f32[1,128,64,1024]{3,1,2,0:T(8,128)} %get-tuple-element.19, f32[128,64]{0,1:T(8,128)S(1)} %reduce_max.38), kind=kLoop, calls=%fused_computation.5 | loop fusion | flops 16769024 | bytes 33619968 | tf_op jit(solution)/shard_map/reduce_sum | solution.py:128
  224.5 0.1 copy.53
  224.6 58.5 %all-reduce = f32[1,128,64]{2,1,0:T(8,128)S(1)} all-reduce(f32[1,128,64]{2,1,0:T(8,128)S(1)} %copy.53), channel_id=7, replica_groups=mesh['seq_0'=4,'seq_1'=4,'batch_0'=4,'batch_1'=2] {'seq_0','seq_1'}, use_global_device_ids=true, to_apply=%region_5.6.clone | all-reduce | flops 8192 | bytes 65536
  283.1 0.1 copy.55
  283.2 0.1 copy.61
  283.4 33.9 %reduce-scatter.3.cloned.1.call-done = f32[1,8,64,512]{3,1,2,0:T(8,128)} async-done(((f32[1,128,64,512]{3,1,2,0:T(8,128)}), f32[1,8,64,512]{3,1,2,0:T(8,128)}) %reduce-scatter.3.cloned.1.call-update) | async-done | bytes 1048592 | tf_op jit(solution)/shard_map/reduce_scatter | solution.py:146
  317.3 1.5 fusion.15
  318.9 0.4 fusion.19
  319.2 0.1 copy.57
  319.4 7.9 %fusion.27 = f32[64,7168]{1,0:T(8,128)S(1)} fusion(bf16[1024,7168]{1,0:T(8,128)(2,1)} %param.25, bf16[8,8,8,128]{3,2,1,0:T(8,128)(2,1)S(1)} %bitcast.377), kind=kOutput, calls=%fused_computation.45 | convolution fusion | flops 939524096 | bytes 16646144 | tf_op jit(solution)/shard_map/dot_general | solution.py:157
  327.2 0.1 convert_add_fusion
  327.4 1.1 add.352
  328.5 1.2 copy-done.2
  329.8 88.2 %all-reduce.3.cloned.1.call-done = f32[64,7168]{1,0:T(8,128)} async-done(((f32[64,7168]{1,0:T(8,128)}), f32[64,7168]{1,0:T(8,128)}) %all-reduce.3.cloned.1.call-update) | async-done | bytes 1835024 | tf_op jit(solution)/shard_map/psum | solution.py:163
  418.0 1.7 multiply_reduce_fusion
  419.7 2.7 multiply_convert_fusion
  423.1 0.1 eq.74
  423.2 0.1 reshape.1086
  423.3 1.6 dynamic-slice_convert_fusion
  425.0 43.8 %all-gather.13.cloned.1.call-done = bf16[512,7168]{1,0:T(8,128)(2,1)} async-done(((bf16[64,7168]{1,0:T(8,128)(2,1)}), bf16[512,7168]{1,0:T(8,128)(2,1)}) %all-gather.13.cloned.1.call-update) | async-done | bytes 7340048 | tf_op jit(solution)/shard_map/all_gather | solution.py:175
  468.8 8.5 %fusion.98 = (f32[512]{0:T(512)S(1)}, f32[512,512]{0,1:T(8,128)S(1)}) fusion(bf16[512,7168]{1,0:T(8,128)(2,1)} %all-gather.13.cloned.1.call-done, bf16[512,7168]{1,0:T(8,128)(2,1)} %param.27), kind=kOutput, calls=%fused_computation.170 | convolution fusion | flops 3758358016 | bytes 15730688 | tf_op jit(solution)/shard_map/rd,vd->rv/dot_general | solution.py:173
  477.3 0.3 copy.58
  477.6 0.2 exponential_reduce_fusion
  477.8 1.6 gather_fusion
  479.5 0.3 select_reduce_fusion
  479.7 9.6 %all-gather.4 = f32[4,3,512]{2,1,0:T(4,128)S(1)} all-gather(f32[1,3,512]{2,1,0:T(4,128)S(1)} %maximum_bitcast_fusion.1), channel_id=2, replica_groups=mesh['seq_0'=4,'seq_1'=4,'batch_0'=4,'batch_1'=2] {'seq_0'}, dimensions={0}, use_global_device_ids=true | all-gather | bytes 30720 | tf_op jit(solution)/shard_map/all_gather | solution.py:43
  489.4 9.5 %all-gather.5 = f32[4,3,512]{2,1,0:T(4,128)S(1)} all-gather(f32[1,3,512]{2,1,0:T(4,128)S(1)} %maximum_bitcast_fusion.2), channel_id=3, replica_groups=mesh['seq_0'=4,'seq_1'=4,'batch_0'=4,'batch_1'=2] {'seq_1'}, dimensions={0}, use_global_device_ids=true | all-gather | bytes 30720 | tf_op jit(solution)/shard_map/all_gather | solution.py:43
  498.9 9.0 %all-gather.6 = f32[4,3,512]{2,1,0:T(4,128)S(1)} all-gather(f32[1,3,512]{2,1,0:T(4,128)S(1)} %maximum_bitcast_fusion.3), channel_id=4, replica_groups=mesh['seq_0'=4,'seq_1'=4,'batch_0'=4,'batch_1'=2] {'batch_0'}, dimensions={0}, use_global_device_ids=true | all-gather | bytes 30720 | tf_op jit(solution)/shard_map/all_gather | solution.py:43
  508.0 10.2 %all-gather.7 = f32[2,3,512]{2,1,0:T(4,128)S(1)} all-gather(f32[1,3,512]{2,1,0:T(4,128)S(1)} %maximum_bitcast_fusion.4), channel_id=5, replica_groups=mesh['seq_0'=4,'seq_1'=4,'batch_0'=4,'batch_1'=2] {'batch_1'}, dimensions={0}, use_global_device_ids=true | all-gather | bytes 18432 | tf_op jit(solution)/shard_map/all_gather | solution.py:43
  518.3 3.5 gather_fusion.1
  521.8 0.1 gather.10
  521.8 0.1 add.384
  521.9 1.1 fusion.89
  (61 shorter events, 0.9 us)
Async XLA Ops:
  7.2 113.3 %copy-start = (bf16[1,1024,512]{2,1,0:T(8,128)(2,1)S(1)}, bf16[1,1024,512]{2,1,0:T(8,128)(2,1)}, u32[]{:S(2)}) copy-start(bf16[1,1024,512]{2,1,0:T(8,128)(2,1)} %param.20) | copy-start | bytes 3145732
  7.2 92.3 %copy-start.5 = (bf16[1,64,512]{2,1,0:T(8,128)(2,1)S(1)}, bf16[1,64,512]{2,1,0:T(8,128)(2,1)}, u32[]{:S(2)}) copy-start(bf16[1,64,512]{2,1,0:T(8,128)(2,1)} %param.22) | copy-start | bytes 196612
  7.2 87.5 %all-gather.11.cloned.1.call-start = ((), (), s32[]{:S(2)}) async-start(), calls=%async_computation.2 | async-start | bytes 11141120 | tf_op jit(solution)/shard_map/all_gather | solution.py:22
  10.8 306.5 %reduce-scatter.3.cloned.1.call-start = ((), (), s32[]{:S(2)}) async-start(), calls=%async_computation.3 | async-start | bytes 17825792 | tf_op jit(solution)/shard_map/reduce_scatter | solution.py:146
  96.5 10.4 %copy-start.8 = (bf16[1,64,64]{2,1,0:T(8,128)(2,1)S(1)}, bf16[1,64,64]{2,1,0:T(8,128)(2,1)}, u32[]{:S(2)}) copy-start(bf16[1,64,64]{2,1,0:T(8,128)(2,1)} %param.23) | copy-start | bytes 24580
  120.5 30.0 %copy-start.3 = (bf16[1,64,128,64]{2,3,1,0:T(8,128)(2,1)S(1)}, bf16[1,64,128,64]{2,3,1,0:T(8,128)(2,1)}, u32[]{:S(2)}) copy-start(bf16[1,64,128,64]{2,3,1,0:T(8,128)(2,1)} %copy.69) | copy-start | bytes 3145732
  120.5 30.0 %copy-start.4 = (bf16[1,1024,64]{1,2,0:T(8,128)(2,1)S(1)}, bf16[1,1024,64]{1,2,0:T(8,128)(2,1)}, u32[]{:S(2)}) copy-start(bf16[1,1024,64]{1,2,0:T(8,128)(2,1)} %param.21) | copy-start | bytes 393220
  206.4 0.7 copy-start.12
  206.4 211.5 %all-reduce.3.cloned.1.call-start = ((), (), s32[]{:S(2)}) async-start(), calls=%async_computation.4 | async-start | bytes 3670016 | tf_op jit(solution)/shard_map/psum | solution.py:163
  209.5 109.3 %copy-start.11 = (bf16[8,512,128]{2,1,0:T(8,128)(2,1)S(1)}, bf16[8,512,128]{2,1,0:T(8,128)(2,1)}, u32[]{:S(2)}) copy-start(bf16[8,512,128]{2,1,0:T(8,128)(2,1)} %param.19) | copy-start | bytes 3145732
  319.3 7.9 %copy-start.6 = (bf16[64,448]{1,0:T(8,128)(2,1)S(1)}, bf16[64,448]{1,0:T(8,128)(2,1)}, u32[]{:S(2)}) copy-start(bf16[64,448]{1,0:T(8,128)(2,1)} %param.24) | copy-start | bytes 172036
  319.3 100.3 %copy-start.7 = (f32[7168]{0:T(1024)S(1)}, f32[7168]{0:T(1024)}, u32[]{:S(2)}) copy-start(f32[7168]{0:T(1024)} %param.26) | copy-start | bytes 86020
  319.4 103.7 %copy-start.9 = (s32[8,64]{1,0:T(8,128)S(1)}, s32[8,64]{1,0:T(8,128)}, u32[]{:S(2)}) copy-start(s32[8,64]{1,0:T(8,128)} %param.29) | copy-start | bytes 6148
  319.4 103.8 %copy-start.10 = (s32[8,64]{1,0:T(8,128)S(1)}, s32[8,64]{1,0:T(8,128)}, u32[]{:S(2)}) copy-start(s32[8,64]{1,0:T(8,128)} %param.28) | copy-start | bytes 6148
  328.5 1.3 copy-start.2
  329.7 139.0 %all-gather.13.cloned.1.call-start = ((), (), s32[]{:S(2)}) async-start(), calls=%async_computation.5 | async-start | bytes 8257536 | tf_op jit(solution)/shard_map/all_gather | solution.py:175
  468.8 54.3 %copy-start.1 = (bf16[1,1024,512]{2,1,0:T(8,128)(2,1)S(1)}, bf16[1,1024,512]{2,1,0:T(8,128)(2,1)}, u32[]{:S(2)}) copy-start(bf16[1,1024,512]{2,1,0:T(8,128)(2,1)} %param.20) | copy-start | bytes 3145732
Sparse Core Ops, SparseCore 0:
  10.9 83.7 all-gather.10
  206.5 110.7 reduce-scatter.2
  329.9 88.0 all-reduce.2
  422.5 46.2 all-gather.12
where the time goes:
time: 530 us
  waiting for transfers between devices  246 us (46%)
  blocking collectives  112 us (21%)
  matrix products  106 us (20%)
  local copies, waits for them, and re-layouts  26 us (5%)
  other arithmetic  23.3 us (4%)
  between operations  16.1 us (3%)
    psum x1, waiting for transfers between devices, body(): stream = lax.psum(branch_term + residual_wide, SEQ)  88.2 us
    all_gather x1, waiting for transfers between devices, sent_together(): lax.all_gather(both, axis, axis=dim, tiled=True)  80.4 us
    unnamed x1, blocking collectives  58.5 us
    all_gather x1, waiting for transfers between devices, body(): lax.all_gather(normed, BATCH, axis=0, tiled=True)  43.8 us
    all_gather x4, blocking collectives, gathered_once(): both, at, found = (lax.all_gather(jnp.concatenate(lines), axis), 0, {})  38.3 us
    reduce_scatter x1, waiting for transfers between devices, body(): lax.psum_scatter(partial_value, SEQ, scatter_dimension=1, tiled=True)  33.9 us
    dot_general x1, matrix products, body(): jnp.einsum('rihc,rtc->rhit', query_all, cache_latent, preferred_element_t...  30 us
    dot_general x1, matrix products, body(): jnp.einsum('rihe,rte->rhit', rope_all, cache_rope, preferred_element_type...  21.9 us
  transfers between devices with their start and end apart: 4, of which 4 were waited for; matrix products, arithmetic and copies ran while one was open for 4% of the time, Pallas kernels for 0%

commit v1 on v0

--- a/solution.py
+++ b/solution.py
@@ -160,7 +160,7 @@
     residual_wide = lax.dynamic_update_slice_in_dim(
         jnp.zeros_like(branch_term), residual.astype(jnp.float32), feature_first, 1
     )
-    stream = lax.psum(branch_term + residual_wide, SEQ)
+    stream = jnp.sum(lax.all_gather(branch_term + residual_wide, SEQ), axis=0)
     square = jnp.sum(stream * stream, axis=1)
     normed = (
         stream * lax.rsqrt(square / stream.shape[1] + norm_epsilon)[:, None] * norm_gain

time: 530 us -> 625 us (1.18)
  waiting for transfers between devices: 246 us -> 334 us
  other arithmetic: 23.3 us -> 31.4 us
    all_gather x0 -> x1, waiting for transfers between devices: none -> 176 us  [body(): stream = jnp.sum(lax.all_gather(branch_term + residual_wide, SEQ), axis=0)]
    psum x1 -> x0, waiting for transfers between devices: 88.2 us -> none  [body(): stream = lax.psum(branch_term + residual_wide, SEQ)]
    reduce_sum x0 -> x1, other arithmetic: none -> 11 us  [body(): stream = jnp.sum(lax.all_gather(branch_term + residual_wide, SEQ), axis=0)]
  transfers between devices with their start and end apart: 4 -> 4, of which waited for: 4 -> 4; matrix products, arithmetic and copies ran while one was open for 4% -> 3% of each run, Pallas kernels for 0% -> 0%
where the time goes in v1:
time: 625 us; the launch traced here: 624 us
  waiting for transfers between devices  334 us (53%)
  blocking collectives  112 us (18%)
  matrix products  106 us (17%)
  other arithmetic  31.4 us (5%)
  local copies, waits for them, and re-layouts  25.1 us (4%)
  between operations  16.1 us (3%)
    all_gather x1, waiting for transfers between devices, body(): stream = jnp.sum(lax.all_gather(branch_term + residual_wide, SEQ), axis=0)  176 us
    all_gather x1, waiting for transfers between devices, sent_together(): lax.all_gather(both, axis, axis=dim, tiled=True)  80.4 us
    unnamed x1, blocking collectives  58.5 us
    all_gather x1, waiting for transfers between devices, body(): lax.all_gather(normed, BATCH, axis=0, tiled=True)  43.9 us
    all_gather x4, blocking collectives, gathered_once(): both, at, found = (lax.all_gather(jnp.concatenate(lines), axis), 0, {})  38.3 us
    reduce_scatter x1, waiting for transfers between devices, body(): lax.psum_scatter(partial_value, SEQ, scatter_dimension=1, tiled=True)  33.9 us
    dot_general x1, matrix products, body(): jnp.einsum('rihc,rtc->rhit', query_all, cache_latent, preferred_element_t...  30 us
    dot_general x1, matrix products, body(): jnp.einsum('rihe,rte->rhit', rope_all, cache_rope, preferred_element_type...  21.9 us
  transfers between devices with their start and end apart: 4, of which 4 were waited for; matrix products, arithmetic and copies ran while one was open for 3% of the time, Pallas kernels for 0%

profile of v1, /device:TPU:1, one launch (start us, length us, event | category | flops | bytes accessed | tf_op | source)
XLA Modules:
  0.0 624.3 jit_solution(15148937121159127965)
XLA Ops:
  7.2 1.0 copy.41
  8.2 1.6 fusion.16
  9.9 0.9 maximum_bitcast_fusion
  11.5 0.7 fusion.88
  12.2 0.2 fusion.39
  12.5 0.2 convolution_add_fusion.5
  12.7 0.2 fusion.99
  12.8 0.2 convolution_add_fusion.4
  13.0 0.2 fusion.100
  13.2 0.2 convolution_add_fusion.3
  13.3 0.2 fusion.101
  13.5 0.2 convolution_add_fusion.2
  13.7 0.2 fusion.102
  13.9 0.2 convolution_add_fusion.1
  14.0 0.2 fusion.17
  14.2 0.1 copy.45
  14.3 80.4 %all-gather.12.cloned.1.call-done = bf16[1,64,128,576]{3,1,0,2:T(8,128)(2,1)} async-done(((bf16[1,64,8,576]{3,1,0,2:T(8,128)(2,1)}), bf16[1,64,128,576]{3,1,0,2:T(8,128)(2,1)}) %all-gather.12.cloned.1.call-update) | async-done | bytes 9437200 | tf_op jit(solution)/shard_map/all_gather | solution.py:22
  94.7 1.8 split.9
  96.5 2.9 copy.69
  99.4 7.5 %fusion.10 = f32[64,128,64]{0,2,1:T(8,128)S(1)} fusion(bf16[1,64,512]{2,1,0:T(8,128)(2,1)S(1)} %copy-done.5, bf16[1,64,128,576]{3,1,0,2:T(8,128)(2,1)} %all-gather.12.cloned.1.call-done), kind=kOutput, calls=%fused_computation.11 | convolution fusion | flops 536870912 | bytes 10551296 | tf_op jit(solution)/shard_map/rihc,rjc->rhij/dot_general | solution.py:116
  106.9 5.8 fusion.97
  112.8 7.7 %split.8 = bf16[1,64,128,512]{3,1,0,2:T(8,128)(2,1)} slice(bf16[1,64,128,576]{3,1,0,2:T(8,128)(2,1)} %all-gather.12.cloned.1.call-done), slice={[0:1], [0:64], [0:128], [0:512]} | slice | bytes 16777216 | tf_op jit(solution)/shard_map/split | solution.py:22
  120.5 30.0 %fusion.12 = f32[64,128,1024]{2,1,0:T(8,128)} fusion(bf16[1,64,128,512]{3,1,0,2:T(8,128)(2,1)} %split.8, bf16[1,1024,512]{2,1,0:T(8,128)(2,1)S(1)} %copy-done), kind=kOutput, calls=%fused_computation.14 | convolution fusion | flops 8589934592 | bytes 42991616 | tf_op jit(solution)/shard_map/rihc,rtc->rhit/dot_general | solution.py:107
  150.5 21.9 %fusion.96 = (f32[128,64]{0,1:T(8,128)S(1)}, f32[1,128,64,1024]{3,1,2,0:T(8,128)}) fusion(f32[64,128,1024]{2,1,0:T(8,128)} %fusion.12, bf16[1,1024,64]{1,2,0:T(8,128)(2,1)S(1)} %copy-done.4, bf16[1,64,128,64]{2,3,1,0:T(8,128)(2,1)S(1)} %copy-done.3, pred[1024]{0:T(1024)(128)(4,1)S(1)} %add_compare_fusion), kind=kOutput, calls=%fused_computation.168 | convolution fusion | flops 1107288064 | bytes 68322304 | tf_op jit(solution)/shard_map/rihe,rte->rhit/dot_general | solution.py:110
  172.5 15.1 %all_to_all.5 = f32[16,1,128,64]{2,3,1,0:T(8,128)S(1)} all-to-all(f32[16,1,128,64]{2,3,1,0:T(8,128)S(1)} %broadcast_in_dim.37), channel_id=1, replica_groups=mesh['seq_0'=4,'seq_1'=4,'batch_0'=4,'batch_1'=2] {'seq_0','seq_1'}, dimensions={0} | all-to-all | bytes 1048576 | tf_op jit(solution)/shard_map/all_to_all | solution.py:27
  187.7 18.7 %fusion.7 = f32[1,128,64,512]{3,1,2,0:T(8,128)} fusion(f32[1,128,64,1024]{3,1,2,0:T(8,128)} %get-tuple-element.19, f32[128,64]{0,1:T(8,128)S(1)} %reduce_max.38, bf16[1,1024,512]{2,1,0:T(8,128)(2,1)S(1)} %copy-done), kind=kOutput, calls=%fused_computation.10 | convolution fusion | flops 8606711808 | bytes 51412992 | tf_op jit(solution)/shard_map/rhit,rtc->rhic/dot_general | solution.py:129
  206.5 0.6 copy-done.12
  207.0 0.6 dynamic-slice.5
  208.3 0.1 constant_dynamic-slice_fusion.1
  208.4 1.0 fusion.24
  209.4 0.1 copy.67
  209.5 14.9 %fusion.1 = f32[128,64]{0,1:T(8,128)S(1)} fusion(f32[1,128,64,1024]{3,1,2,0:T(8,128)} %get-tuple-element.19, f32[128,64]{0,1:T(8,128)S(1)} %reduce_max.38), kind=kLoop, calls=%fused_computation.5 | loop fusion | flops 16769024 | bytes 33619968 | tf_op jit(solution)/shard_map/reduce_sum | solution.py:128
  224.5 0.1 copy.53
  224.6 58.5 %all-reduce = f32[1,128,64]{2,1,0:T(8,128)S(1)} all-reduce(f32[1,128,64]{2,1,0:T(8,128)S(1)} %copy.53), channel_id=7, replica_groups=mesh['seq_0'=4,'seq_1'=4,'batch_0'=4,'batch_1'=2] {'seq_0','seq_1'}, use_global_device_ids=true, to_apply=%region_5.6.clone | all-reduce | flops 8192 | bytes 65536
  283.1 0.1 copy.55
  283.2 0.1 copy.61
  283.4 33.9 %reduce-scatter.3.cloned.1.call-done = f32[1,8,64,512]{3,1,2,0:T(8,128)} async-done(((f32[1,128,64,512]{3,1,2,0:T(8,128)}), f32[1,8,64,512]{3,1,2,0:T(8,128)}) %reduce-scatter.3.cloned.1.call-update) | async-done | bytes 1048592 | tf_op jit(solution)/shard_map/reduce_scatter | solution.py:146
  317.3 1.5 fusion.15
  318.9 0.4 fusion.19
  319.2 0.1 copy.57
  319.3 7.9 %fusion.27 = f32[64,7168]{1,0:T(8,128)S(1)} fusion(bf16[1024,7168]{1,0:T(8,128)(2,1)} %param.25, bf16[8,8,8,128]{3,2,1,0:T(8,128)(2,1)S(1)} %bitcast.381), kind=kOutput, calls=%fused_computation.45 | convolution fusion | flops 939524096 | bytes 16646144 | tf_op jit(solution)/shard_map/dot_general | solution.py:157
  327.2 0.1 add_bitcast_fusion
  327.3 1.1 add.350
  328.4 1.3 copy-done.2
  329.8 175.6 %all-gather.14.cloned.1.call-done = f32[16,64,7168]{2,1,0:T(8,128)} async-done(((f32[1,64,7168]{2,1,0:T(8,128)}), f32[16,64,7168]{2,1,0:T(8,128)}) %all-gather.14.cloned.1.call-update) | async-done | bytes 29360144 | tf_op jit(solution)/shard_map/all_gather | solution.py:163
  505.4 11.0 %reduce_sum.73 = f32[64,7168]{1,0:T(8,128)S(1)} reduce(f32[16,64,7168]{2,1,0:T(8,128)} %all-gather.14.cloned.1.call-done, f32[]{:T(128)} %constant.15.clone.1), dimensions={0}, to_apply=%region_7.8 | reduce | flops 6881280 | bytes 31195140 | tf_op jit(solution)/shard_map/reduce_sum | solution.py:163
  516.5 0.2 multiply_reduce_fusion
  516.7 1.2 multiply_convert_fusion
  518.6 0.1 eq.74
  518.7 0.1 reshape.1088
  518.8 0.7 dynamic-slice_convert_fusion
  519.6 43.9 %all-gather.16.cloned.1.call-done = bf16[512,7168]{1,0:T(8,128)(2,1)} async-done(((bf16[64,7168]{1,0:T(8,128)(2,1)}), bf16[512,7168]{1,0:T(8,128)(2,1)}) %all-gather.16.cloned.1.call-update) | async-done | bytes 7340048 | tf_op jit(solution)/shard_map/all_gather | solution.py:175
  563.4 8.5 %fusion.98 = (f32[512]{0:T(512)S(1)}, f32[512,512]{0,1:T(8,128)S(1)}) fusion(bf16[512,7168]{1,0:T(8,128)(2,1)} %all-gather.16.cloned.1.call-done, bf16[512,7168]{1,0:T(8,128)(2,1)} %param.27), kind=kOutput, calls=%fused_computation.170 | convolution fusion | flops 3758358016 | bytes 15730688 | tf_op jit(solution)/shard_map/rd,vd->rv/dot_general | solution.py:173
  572.0 0.3 copy.58
  572.3 0.2 exponential_reduce_fusion
  572.5 1.6 gather_fusion
  574.1 0.3 select_reduce_fusion
  574.4 9.6 %all-gather.4 = f32[4,3,512]{2,1,0:T(4,128)S(1)} all-gather(f32[1,3,512]{2,1,0:T(4,128)S(1)} %maximum_bitcast_fusion.1), channel_id=2, replica_groups=mesh['seq_0'=4,'seq_1'=4,'batch_0'=4,'batch_1'=2] {'seq_0'}, dimensions={0}, use_global_device_ids=true | all-gather | bytes 30720 | tf_op jit(solution)/shard_map/all_gather | solution.py:43
  584.1 9.5 %all-gather.5 = f32[4,3,512]{2,1,0:T(4,128)S(1)} all-gather(f32[1,3,512]{2,1,0:T(4,128)S(1)} %maximum_bitcast_fusion.2), channel_id=3, replica_groups=mesh['seq_0'=4,'seq_1'=4,'batch_0'=4,'batch_1'=2] {'seq_1'}, dimensions={0}, use_global_device_ids=true | all-gather | bytes 30720 | tf_op jit(solution)/shard_map/all_gather | solution.py:43
  593.7 9.0 %all-gather.6 = f32[4,3,512]{2,1,0:T(4,128)S(1)} all-gather(f32[1,3,512]{2,1,0:T(4,128)S(1)} %maximum_bitcast_fusion.3), channel_id=4, replica_groups=mesh['seq_0'=4,'seq_1'=4,'batch_0'=4,'batch_1'=2] {'batch_0'}, dimensions={0}, use_global_device_ids=true | all-gather | bytes 30720 | tf_op jit(solution)/shard_map/all_gather | solution.py:43
  602.7 10.2 %all-gather.7 = f32[2,3,512]{2,1,0:T(4,128)S(1)} all-gather(f32[1,3,512]{2,1,0:T(4,128)S(1)} %maximum_bitcast_fusion.4), channel_id=5, replica_groups=mesh['seq_0'=4,'seq_1'=4,'batch_0'=4,'batch_1'=2] {'batch_1'}, dimensions={0}, use_global_device_ids=true | all-gather | bytes 18432 | tf_op jit(solution)/shard_map/all_gather | solution.py:43
  612.9 3.5 gather_fusion.1
  616.4 0.1 gather.10
  616.6 1.1 fusion.89
  (62 shorter events, 1.0 us)
Async XLA Ops:
  7.2 113.3 %copy-start = (bf16[1,1024,512]{2,1,0:T(8,128)(2,1)S(1)}, bf16[1,1024,512]{2,1,0:T(8,128)(2,1)}, u32[]{:S(2)}) copy-start(bf16[1,1024,512]{2,1,0:T(8,128)(2,1)} %param.20) | copy-start | bytes 3145732
  7.2 92.3 %copy-start.5 = (bf16[1,64,512]{2,1,0:T(8,128)(2,1)S(1)}, bf16[1,64,512]{2,1,0:T(8,128)(2,1)}, u32[]{:S(2)}) copy-start(bf16[1,64,512]{2,1,0:T(8,128)(2,1)} %param.22) | copy-start | bytes 196612
  7.2 87.5 %all-gather.12.cloned.1.call-start = ((), (), s32[]{:S(2)}) async-start(), calls=%async_computation.2 | async-start | bytes 11141120 | tf_op jit(solution)/shard_map/all_gather | solution.py:22
  10.8 306.5 %reduce-scatter.3.cloned.1.call-start = ((), (), s32[]{:S(2)}) async-start(), calls=%async_computation.3 | async-start | bytes 17825792 | tf_op jit(solution)/shard_map/reduce_scatter | solution.py:146
  96.5 10.4 %copy-start.8 = (bf16[1,64,64]{2,1,0:T(8,128)(2,1)S(1)}, bf16[1,64,64]{2,1,0:T(8,128)(2,1)}, u32[]{:S(2)}) copy-start(bf16[1,64,64]{2,1,0:T(8,128)(2,1)} %param.23) | copy-start | bytes 24580
  120.5 30.0 %copy-start.3 = (bf16[1,64,128,64]{2,3,1,0:T(8,128)(2,1)S(1)}, bf16[1,64,128,64]{2,3,1,0:T(8,128)(2,1)}, u32[]{:S(2)}) copy-start(bf16[1,64,128,64]{2,3,1,0:T(8,128)(2,1)} %copy.69) | copy-start | bytes 3145732
  120.5 30.0 %copy-start.4 = (bf16[1,1024,64]{1,2,0:T(8,128)(2,1)S(1)}, bf16[1,1024,64]{1,2,0:T(8,128)(2,1)}, u32[]{:S(2)}) copy-start(bf16[1,1024,64]{1,2,0:T(8,128)(2,1)} %param.21) | copy-start | bytes 393220
  206.4 0.7 copy-start.12
  206.4 299.0 %all-gather.14.cloned.1.call-start = ((), (), s32[]{:S(2)}) async-start(), calls=%async_computation.4 | async-start | bytes 31195136 | tf_op jit(solution)/shard_map/all_gather | solution.py:163
  209.5 109.3 %copy-start.11 = (bf16[8,512,128]{2,1,0:T(8,128)(2,1)S(1)}, bf16[8,512,128]{2,1,0:T(8,128)(2,1)}, u32[]{:S(2)}) copy-start(bf16[8,512,128]{2,1,0:T(8,128)(2,1)} %param.19) | copy-start | bytes 3145732
  319.3 7.9 %copy-start.6 = (bf16[64,448]{1,0:T(8,128)(2,1)S(1)}, bf16[64,448]{1,0:T(8,128)(2,1)}, u32[]{:S(2)}) copy-start(bf16[64,448]{1,0:T(8,128)(2,1)} %param.24) | copy-start | bytes 172036
  328.4 1.3 copy-start.2
  329.7 187.0 %copy-start.7 = (f32[7168]{0:T(1024)S(1)}, f32[7168]{0:T(1024)}, u32[]{:S(2)}) copy-start(f32[7168]{0:T(1024)} %param.26) | copy-start | bytes 86020
  329.7 188.8 %copy-start.9 = (s32[8,64]{1,0:T(8,128)S(1)}, s32[8,64]{1,0:T(8,128)}, u32[]{:S(2)}) copy-start(s32[8,64]{1,0:T(8,128)} %param.29) | copy-start | bytes 6148
  329.7 188.9 %copy-start.10 = (s32[8,64]{1,0:T(8,128)S(1)}, s32[8,64]{1,0:T(8,128)}, u32[]{:S(2)}) copy-start(s32[8,64]{1,0:T(8,128)} %param.28) | copy-start | bytes 6148
  329.8 233.7 %all-gather.16.cloned.1.call-start = ((), (), s32[]{:S(2)}) async-start(), calls=%async_computation.5 | async-start | bytes 8257536 | tf_op jit(solution)/shard_map/all_gather | solution.py:175
  563.4 54.3 %copy-start.1 = (bf16[1,1024,512]{2,1,0:T(8,128)(2,1)S(1)}, bf16[1,1024,512]{2,1,0:T(8,128)(2,1)}, u32[]{:S(2)}) copy-start(bf16[1,1024,512]{2,1,0:T(8,128)(2,1)} %param.20) | copy-start | bytes 3145732
Sparse Core Ops, SparseCore 0:
  10.9 83.7 all-gather.11
  206.5 110.7 reduce-scatter.2
  329.8 175.5 all-gather.13
  518.0 45.3 all-gather.15
